TPU v7x, 128 devices: a whole 4x4x4 slice. The times are simulated.
128 devices in a mesh: member: 2 (over y_hi), gridy: 8 (over x, core), gridx: 8 (over z, y_lo).
Axes of the slice: x: 4, y: 4 (y_hi: 2, y_lo: 2; y = y_hi * 2 + y_lo), z: 4, core: 2. Of those that a mesh axis runs over, the one named last changes fastest.
Arguments:
- temp: float32 [4, 4, 512, 2048], P('member', None, 'gridy', 'gridx'), may hold values from -6 to 6
- salt: float32 [4, 4, 512, 2048], P('member', None, 'gridy', 'gridx'), may hold values from -6 to 6
- uvel: float32 [4, 4, 512, 2048], P('member', None, 'gridy', 'gridx'), may hold values from -3 to 3
- vvel: float32 [4, 4, 512, 2048], P('member', None, 'gridy', 'gridx'), may hold values from -3 to 3
- eta: float32 [4, 512, 2048], P('member', 'gridy', 'gridx'), may hold values from -6 to 6
- land_mask: int32 [512, 2048], P('gridy', 'gridx'), may hold values 0 or 1
- clone_source: int32 [4], P('member'), may hold values from 0 to 3
Outputs:
- new_temp: float32 [4, 4, 512, 2048], P('member', None, 'gridy', 'gridx')
- new_salt: float32 [4, 4, 512, 2048], P('member', None, 'gridy', 'gridx')
- new_uvel: float32 [4, 4, 512, 2048], P('member', None, 'gridy', 'gridx')
- new_vvel: float32 [4, 4, 512, 2048], P('member', None, 'gridy', 'gridx')
- new_eta: float32 [4, 512, 2048], P('member', 'gridy', 'gridx')
- overturning: float32 [4, 4, 512], P('member', None, 'gridy')
- clone_weight: float32 [4], P('member')
All inputs are finite; a program needn't handle non-finite values. No bound on the sum of `land_mask` on one device may be relied on, other than what follows from the above.
Results may differ from a plain program's by a relative error of at most 0.0001.
Values sent between devices are 32-bit elements; how exact they have to be, the bound alone decides.
A program may use at most 128 MiB of HBM per device.

v0:
```python
import jax
import jax.numpy as jnp
from jax import lax
from jax.sharding import PartitionSpec as P

STEPS = 2
ITERS = 3
ALPHA_T = 0.8
BETA_S = 0.6
PRESS_K = 0.25
STEP_DT = 0.1
KAPPA = 0.1
VISCOSITY = 0.1
DRAG_K = 0.05
CORI_K = 1.0
SURF_C = 4.0
DIV_K = 0.5
GRAV_K = 0.5


def padded_2(block, sides, width):
    for axis, dim in sides:
        count = lax.axis_size(axis)
        forward = [(i, i + 1) for i in range(count - 1)]
        forward.append((count - 1, 0))
        backward = [(target, source) for source, target in forward]
        low = lax.ppermute(
            lax.slice_in_dim(block, block.shape[dim] - width, None, axis=dim), axis, forward
        )
        high = lax.ppermute(lax.slice_in_dim(block, 0, width, axis=dim), axis, backward)
        block = jnp.concatenate([low, block, high], axis=dim)
    return block


def tree_sum(values, axes):
    for axis in axes:
        count = lax.axis_size(axis)
        step = 1
        while step < count:
            pairs = [(i, i ^ step) for i in range(count)]
            values = values + lax.ppermute(values, axis, pairs)
            step *= 2
    return values


def pressure(temp, salt):
    return PRESS_K * jnp.cumsum(BETA_S * salt - ALPHA_T * temp, axis=-3)


def split_rims(padded, south_keep, north_keep):
    east_side = padded[..., 1:-1, 2:]
    west_side = padded[..., 1:-1, :-2]
    north_side = padded[..., 2:, 1:-1]
    south_side = padded[..., :-2, 1:-1]
    north_side = north_side.at[..., -1, :].multiply(north_keep)
    south_side = south_side.at[..., 0, :].multiply(south_keep)
    return (east_side, west_side, north_side, south_side)


def volume_sides(fields, south_keep, north_keep):
    padded = padded_2(jnp.stack(fields), (("gridy", 3), ("gridx", 4)), 1)
    return split_rims(padded, south_keep, north_keep)


def surface_sides(fields, south_keep, north_keep):
    padded = padded_2(jnp.stack(fields), (("gridy", 2), ("gridx", 3)), 1)
    return split_rims(padded, south_keep, north_keep)


def surface_apply(field, south_keep, north_keep):
    east_side, west_side, north_side, south_side = surface_sides((field,), south_keep, north_keep)
    return (1.0 + 4.0 * SURF_C) * field - SURF_C * (
        east_side[0] + west_side[0] + north_side[0] + south_side[0]
    )


def member_total(values):
    return jnp.sum(values, axis=(1, 2))


def squared_norm(residual):
    return tree_sum(member_total(residual * residual), ("gridy", "gridx"))


def widen(values):
    return values[:, None, None]


def surface_solve(rhs, south_keep, north_keep):
    solution = jnp.zeros_like(rhs)
    residual = rhs
    direction = rhs
    norm_now = squared_norm(residual)
    for count in range(ITERS):
        image = surface_apply(direction, south_keep, north_keep)
        alpha = norm_now / tree_sum(member_total(direction * image), ("gridy", "gridx"))
        solution = solution + widen(alpha) * direction
        residual = residual - widen(alpha) * image
        norm_next = squared_norm(residual)
        direction = residual + widen(norm_next / norm_now) * direction
        norm_now = norm_next
    return solution


def shards(temp, salt, uvel, vvel, eta, land_mask, clone_source):
    levels = temp.shape[1]
    rows = temp.shape[2]
    cols = temp.shape[3]
    ocean = land_mask.astype(jnp.float32)
    tile_row = lax.axis_index("gridy")
    tile_count = lax.axis_size("gridy")
    total_rows = rows * tile_count
    total_cols = cols * lax.axis_size("gridx")
    south_keep = (tile_row > 0).astype(jnp.float32)
    north_keep = (tile_row < tile_count - 1).astype(jnp.float32)
    latitude = (tile_row * rows + jnp.arange(rows, dtype=jnp.int32)).astype(jnp.float32) + 0.5
    coriolis = (CORI_K * (2.0 * latitude / total_rows - 1.0))[:, None]
    for count in range(STEPS):
        press = pressure(temp, salt)
        east_side, west_side, north_side, south_side = volume_sides(
            (temp, salt, uvel, vvel, press), south_keep, north_keep
        )
        lap_temp = east_side[0] + west_side[0] + north_side[0] + south_side[0] - 4.0 * temp
        lap_salt = east_side[1] + west_side[1] + north_side[1] + south_side[1] - 4.0 * salt
        lap_uvel = east_side[2] + west_side[2] + north_side[2] + south_side[2] - 4.0 * uvel
        lap_vvel = east_side[3] + west_side[3] + north_side[3] + south_side[3] - 4.0 * vvel
        temp_next = ocean * (
            temp
            - STEP_DT
            * 0.5
            * (uvel * (east_side[0] - west_side[0]) + vvel * (north_side[0] - south_side[0]))
            + KAPPA * lap_temp
        )
        salt_next = ocean * (
            salt
            - STEP_DT
            * 0.5
            * (uvel * (east_side[1] - west_side[1]) + vvel * (north_side[1] - south_side[1]))
            + KAPPA * lap_salt
        )
        ustar = ocean * (
            uvel
            + STEP_DT * (coriolis * vvel - 0.5 * (east_side[4] - west_side[4]) - DRAG_K * uvel)
            + VISCOSITY * lap_uvel
        )
        vstar = ocean * (
            vvel
            + STEP_DT * (-coriolis * uvel - 0.5 * (north_side[4] - south_side[4]) - DRAG_K * vvel)
            + VISCOSITY * lap_vvel
        )
        trans_u = jnp.sum(ustar, axis=1)
        trans_v = jnp.sum(vstar, axis=1)
        east_t, west_t, north_t, south_t = surface_sides((trans_u, trans_v), south_keep, north_keep)
        rhs = eta - DIV_K * 0.5 * (east_t[0] - west_t[0] + (north_t[1] - south_t[1]))
        eta = surface_solve(rhs, south_keep, north_keep)
        east_e, west_e, north_e, south_e = surface_sides((eta,), south_keep, north_keep)
        uvel = ocean * (ustar - GRAV_K * 0.5 * (east_e[0] - west_e[0])[:, None])
        vvel = ocean * (vstar - GRAV_K * 0.5 * (north_e[0] - south_e[0])[:, None])
        temp = temp_next
        salt = salt_next
    zonal_scale = 1.0 / jnp.sqrt(jnp.float32(total_cols))
    score_scale = 1.0 / jnp.sqrt(jnp.float32(levels * total_rows))
    lat_weight = latitude / total_rows
    zonal_local = jnp.sum(vvel, axis=3)
    zonal_whole = tree_sum(zonal_local, ("gridx",))
    overturn = jnp.cumsum(zonal_whole, axis=1) * zonal_scale
    score = tree_sum(jnp.sum(overturn * lat_weight, axis=(1, 2)) * score_scale, ("gridy",))
    state_stack = jnp.stack((temp, salt, uvel, vvel))
    every_state, every_eta, every_score = (
        lax.all_gather(state_stack, "member", axis=1, tiled=True),
        lax.all_gather(eta, "member", axis=0, tiled=True),
        lax.all_gather(score, "member", axis=0, tiled=True),
    )
    picked = jnp.take(every_state, clone_source, axis=1)
    new_eta = jnp.take(every_eta, clone_source, axis=0)
    clone_weight = jnp.take(every_score, clone_source, axis=0) - jnp.mean(every_score)
    return (picked[0], picked[1], picked[2], picked[3], new_eta, overturn, clone_weight)


def solution(mesh):
    in_specs = (
        P("member", None, "gridy", "gridx"),
        P("member", None, "gridy", "gridx"),
        P("member", None, "gridy", "gridx"),
        P("member", None, "gridy", "gridx"),
        P("member", "gridy", "gridx"),
        P("gridy", "gridx"),
        P("member"),
    )
    out_specs = (
        P("member", None, "gridy", "gridx"),
        P("member", None, "gridy", "gridx"),
        P("member", None, "gridy", "gridx"),
        P("member", None, "gridy", "gridx"),
        P("member", "gridy", "gridx"),
        P("member", None, "gridy"),
        P("member"),
    )
    return jax.shard_map(shards, mesh=mesh, in_specs=in_specs, out_specs=out_specs, check_vma=False)
```

profile of v0, /device:TPU:1, one launch (start us, length us, event | category | flops | bytes accessed | tf_op | source)
XLA Modules:
  0.0 543.2 jit_solution(18020476195742906736)
XLA Ops:
  43.5 4.2 collective-permute-start.5
  61.9 3.9 collective-permute-start.16
  67.9 4.2 collective-permute-start.18
  91.1 5.9 %collective-permute-start.24 = (f32[2]{0:T(128)S(1)}, f32[2]{0:T(128)S(1)}, u32[]{:S(2)}, u32[]{:S(2)}) collective-permute-start(f32[2]{0:T(128)S(1)} %get-tuple-element.322), channel_id=1, source_target_pairs={{0,8},{8,0},{16,24},{24,16},{32,40},{40,32},{48,56},{56,48},{1,9},... | collective-permute-start | bytes 32 | tf_op jit(solution)/shard_map/ppermute | solution.py:41
  113.0 6.0 %collective-permute-start.31 = (f32[1,2,1,256]{3,2,1,0:T(1,128)S(1)}, f32[1,2,1,256]{3,2,1,0:T(1,128)S(1)}, u32[]{:S(2)}, u32[]{:S(2)}) collective-permute-start(f32[1,2,1,256]{3,2,1,0:T(1,128)S(1)} %get-tuple-element.409), channel_id=1, source_target_pairs={{8,0},{16,8},{24,16},{32,24},{40,32},{48,40},{56,48},{0,56},{9,1},... | collective-permute-start | bytes 6152 | tf_op jit(solution)/shard_map/ppermute | solution.py:30
  125.9 4.2 collective-permute-start.34
  133.7 3.6 collective-permute-done.36
  146.1 6.1 %collective-permute-start.40 = (f32[2]{0:T(128)S(1)}, f32[2]{0:T(128)S(1)}, u32[]{:S(2)}, u32[]{:S(2)}) collective-permute-start(f32[2]{0:T(128)S(1)} %multiply_reduce_fusion.5), channel_id=1, source_target_pairs={{0,8},{8,0},{16,24},{24,16},{32,40},{40,32},{48,56},{56,48},{1,9},... | collective-permute-start | bytes 32 | tf_op jit(solution)/shard_map/ppermute | solution.py:41
  155.7 3.6 collective-permute-done.42
  168.6 6.1 %collective-permute-start.47 = (f32[1,2,1,256]{3,2,1,0:T(1,128)S(1)}, f32[1,2,1,256]{3,2,1,0:T(1,128)S(1)}, u32[]{:S(2)}, u32[]{:S(2)}) collective-permute-start(f32[1,2,1,256]{3,2,1,0:T(1,128)S(1)} %get-tuple-element.405), channel_id=1, source_target_pairs={{8,0},{16,8},{24,16},{32,24},{40,32},{48,40},{56,48},{0,56},{9,1},... | collective-permute-start | bytes 6152 | tf_op jit(solution)/shard_map/ppermute | solution.py:30
  174.7 3.6 bitcast_dynamic-update-slice_fusion.3
  207.4 5.7 %collective-permute-start.56 = (f32[1,2,1,256]{3,2,1,0:T(1,128)S(1)}, f32[1,2,1,256]{3,2,1,0:T(1,128)S(1)}, u32[]{:S(2)}, u32[]{:S(2)}) collective-permute-start(f32[1,2,1,256]{3,2,1,0:T(1,128)S(1)} %get-tuple-element.401), channel_id=1, source_target_pairs={{0,8},{8,16},{16,24},{24,32},{32,40},{40,48},{48,56},{56,0},{1,9},... | collective-permute-start | bytes 6152 | tf_op jit(solution)/shard_map/ppermute | solution.py:27
  228.0 4.1 collective-permute-start.61
  240.9 3.9 collective-permute-start.62
  264.9 3.7 collective-permute-start.65
  279.2 3.7 collective-permute-start.75
  284.8 3.6 collective-permute-start.76
  294.3 3.8 collective-permute-start.78
  316.1 6.5 %collective-permute-start.84 = (f32[2]{0:T(128)S(1)}, f32[2]{0:T(128)S(1)}, u32[]{:S(2)}, u32[]{:S(2)}) collective-permute-start(f32[2]{0:T(128)S(1)} %get-tuple-element.307), channel_id=1, source_target_pairs={{0,8},{8,0},{16,24},{24,16},{32,40},{40,32},{48,56},{56,48},{1,9},... | collective-permute-start | bytes 32 | tf_op jit(solution)/shard_map/ppermute | solution.py:41
  339.0 6.1 %collective-permute-start.91 = (f32[1,2,1,256]{3,2,1,0:T(1,128)S(1)}, f32[1,2,1,256]{3,2,1,0:T(1,128)S(1)}, u32[]{:S(2)}, u32[]{:S(2)}) collective-permute-start(f32[1,2,1,256]{3,2,1,0:T(1,128)S(1)} %get-tuple-element.395), channel_id=1, source_target_pairs={{8,0},{16,8},{24,16},{32,24},{40,32},{48,40},{56,48},{0,56},{9,1},... | collective-permute-start | bytes 6152 | tf_op jit(solution)/shard_map/ppermute | solution.py:30
  377.6 6.1 %collective-permute-start.100 = (f32[2]{0:T(128)S(1)}, f32[2]{0:T(128)S(1)}, u32[]{:S(2)}, u32[]{:S(2)}) collective-permute-start(f32[2]{0:T(128)S(1)} %multiply_reduce_fusion), channel_id=1, source_target_pairs={{0,8},{8,0},{16,24},{24,16},{32,40},{40,32},{48,56},{56,48},{1,9},... | collective-permute-start | bytes 32 | tf_op jit(solution)/shard_map/ppermute | solution.py:41
  401.6 6.1 %collective-permute-start.107 = (f32[1,2,1,256]{3,2,1,0:T(1,128)S(1)}, f32[1,2,1,256]{3,2,1,0:T(1,128)S(1)}, u32[]{:S(2)}, u32[]{:S(2)}) collective-permute-start(f32[1,2,1,256]{3,2,1,0:T(1,128)S(1)} %get-tuple-element.391), channel_id=1, source_target_pairs={{8,0},{16,8},{24,16},{32,24},{40,32},{48,40},{56,48},{0,56},{9,1},... | collective-permute-start | bytes 6152 | tf_op jit(solution)/shard_map/ppermute | solution.py:30
  409.6 3.6 collective-permute-start.108
  419.2 3.7 collective-permute-start.110
  426.1 3.9 collective-permute-done.112
  440.4 6.1 %collective-permute-start.117 = (f32[1,2,1,256]{3,2,1,0:T(1,128)S(1)}, f32[1,2,1,256]{3,2,1,0:T(1,128)S(1)}, u32[]{:S(2)}, u32[]{:S(2)}) collective-permute-start(f32[1,2,1,256]{3,2,1,0:T(1,128)S(1)} %get-tuple-element.388), channel_id=1, source_target_pairs={{8,0},{16,8},{24,16},{32,24},{40,32},{48,40},{56,48},{0,56},{9,1},... | collective-permute-start | bytes 6152 | tf_op jit(solution)/shard_map/ppermute | solution.py:30
  472.0 6.0 %all_gather.10 = f32[4,64,256]{2,1,0:T(8,128)S(1)} all-gather(f32[2,64,256]{2,1,0:T(8,128)S(1)} %copy-done.28), channel_id=1, replica_groups=mesh['member'=2,'gridy'=8,'gridx'=8] {'member'}, dimensions={0}, use_global_device_ids=true | all-gather | bytes 393216 | tf_op jit(solution)/shard_map/all_gather | solution.py:171
  478.6 9.3 %collective-permute-start.123 = (f32[2]{0:T(128)S(1)}, f32[2]{0:T(128)S(1)}, u32[]{:S(2)}, u32[]{:S(2)}) collective-permute-start(f32[2]{0:T(128)S(1)} %broadcast_multiply_fusion.9), channel_id=1, source_target_pairs={{0,8},{8,0},{16,24},{24,16},{32,40},{40,32},{48,56},{56,48},{1,9},... | collective-permute-start | bytes 32 | tf_op jit(solution)/shard_map/ppermute | solution.py:41
  491.5 4.3 collective-permute-done.125
  496.5 5.8 %all-reduce = f32[4]{0:T(128)S(1)} all-reduce(f32[4]{0:T(128)S(1)} %add_dynamic-update-slice_fusion), channel_id=1, replica_groups=mesh['member'=2,'gridy'=8,'gridx'=8] {'member'}, use_global_device_ids=true, to_apply=%add | all-reduce | flops 4 | bytes 32
  505.4 23.3 %all-gather.2.cloned.1.call-done = f32[4,4,4,64,256]{4,3,2,1,0:T(8,128)} async-done(((f32[4,2,4,64,256]{4,3,2,1,0:T(8,128)}), f32[4,4,4,64,256]{4,3,2,1,0:T(8,128)}) %all-gather.2.cloned.1.call-update) | async-done | bytes 4194320 | tf_op jit(solution)/shard_map/all_gather | solution.py:170
  528.6 4.3 gather_fusion
  (568 shorter events, 352.0 us)
Async XLA Ops:
  7.2 521.5 %all-gather.2.cloned.1.call-start = ((), (), s32[]{:S(2)}) async-start(), calls=%async_computation | async-start | bytes 6291456 | tf_op jit(solution)/shard_map/all_gather | solution.py:170
  19.8 14.3 %collective-permute-start.3 = (f32[5,2,4,66,1]{3,2,4,1,0:T(4,128)S(1)}, f32[5,2,4,66,1]{3,2,4,1,0:T(4,128)S(1)}, u32[]{:S(2)}, u32[]{:S(2)}) collective-permute-start(f32[5,2,4,66,1]{3,2,4,1,0:T(4,128)S(1)} %copy.16), channel_id=1, source_target_pairs={{0,1},{1,2},{2,3},{3,4},{4,5},{5,6},{6,7},{7,0},{8,9},{9,10},{10,1... | collective-permute-start | bytes 31688 | tf_op jit(solution)/shard_map/ppermute | solution.py:27
  23.0 12.7 %collective-permute-start.2 = (f32[5,2,4,66,1]{3,2,4,1,0:T(4,128)S(1)}, f32[5,2,4,66,1]{3,2,4,1,0:T(4,128)S(1)}, u32[]{:S(2)}, u32[]{:S(2)}) collective-permute-start(f32[5,2,4,66,1]{3,2,4,1,0:T(4,128)S(1)} %copy.14), channel_id=1, source_target_pairs={{1,0},{2,1},{3,2},{4,3},{5,4},{6,5},{7,6},{0,7},{9,8},{10,9},{11,1... | collective-permute-start | bytes 31688 | tf_op jit(solution)/shard_map/ppermute | solution.py:30
  49.1 6.2 %collective-permute-start.7 = (f32[2,2,66,1]{3,2,1,0:T(8,128)S(1)}, f32[2,2,66,1]{3,2,1,0:T(8,128)S(1)}, u32[]{:S(2)}, u32[]{:S(2)}) collective-permute-start(f32[2,2,66,1]{3,2,1,0:T(8,128)S(1)} %get-tuple-element.356), channel_id=1, source_target_pairs={{0,1},{1,2},{2,3},{3,4},{4,5},{5,6},{6,7},{7,0},{8,9},{9,10},{10,1... | collective-permute-start | bytes 3176 | tf_op jit(solution)/shard_map/ppermute | solution.py:27
  49.1 6.9 %collective-permute-start.6 = (f32[2,2,66,1]{3,2,1,0:T(8,128)S(1)}, f32[2,2,66,1]{3,2,1,0:T(8,128)S(1)}, u32[]{:S(2)}, u32[]{:S(2)}) collective-permute-start(f32[2,2,66,1]{3,2,1,0:T(8,128)S(1)} %get-tuple-element.355), channel_id=1, source_target_pairs={{1,0},{2,1},{3,2},{4,3},{5,4},{6,5},{7,6},{0,7},{9,8},{10,9},{11,1... | collective-permute-start | bytes 3176 | tf_op jit(solution)/shard_map/ppermute | solution.py:30
  61.8 5.7 %collective-permute-start.17 = (f32[1,2,66,1]{3,2,1,0:T(8,128)S(1)}, f32[1,2,66,1]{3,2,1,0:T(8,128)S(1)}, u32[]{:S(2)}, u32[]{:S(2)}) collective-permute-start(f32[1,2,66,1]{3,2,1,0:T(8,128)S(1)} %get-tuple-element.380), channel_id=1, source_target_pairs={{0,1},{1,2},{2,3},{3,4},{4,5},{5,6},{6,7},{7,0},{8,9},{9,10},{10,1... | collective-permute-start | bytes 1592 | tf_op jit(solution)/shard_map/ppermute | solution.py:27
  61.9 5.7 %collective-permute-start.16 = (f32[1,2,66,1]{3,2,1,0:T(8,128)S(1)}, f32[1,2,66,1]{3,2,1,0:T(8,128)S(1)}, u32[]{:S(2)}, u32[]{:S(2)}) collective-permute-start(f32[1,2,66,1]{3,2,1,0:T(8,128)S(1)} %get-tuple-element.379), channel_id=1, source_target_pairs={{1,0},{2,1},{3,2},{4,3},{5,4},{6,5},{7,6},{0,7},{9,8},{10,9},{11,1... | collective-permute-start | bytes 1592 | tf_op jit(solution)/shard_map/ppermute | solution.py:30
  91.1 6.7 %collective-permute-start.24 = (f32[2]{0:T(128)S(1)}, f32[2]{0:T(128)S(1)}, u32[]{:S(2)}, u32[]{:S(2)}) collective-permute-start(f32[2]{0:T(128)S(1)} %get-tuple-element.322), channel_id=1, source_target_pairs={{0,8},{8,0},{16,24},{24,16},{32,40},{40,32},{48,56},{56,48},{1,9},... | collective-permute-start | bytes 32 | tf_op jit(solution)/shard_map/ppermute | solution.py:41
  113.0 7.2 %collective-permute-start.31 = (f32[1,2,1,256]{3,2,1,0:T(1,128)S(1)}, f32[1,2,1,256]{3,2,1,0:T(1,128)S(1)}, u32[]{:S(2)}, u32[]{:S(2)}) collective-permute-start(f32[1,2,1,256]{3,2,1,0:T(1,128)S(1)} %get-tuple-element.409), channel_id=1, source_target_pairs={{8,0},{16,8},{24,16},{32,24},{40,32},{48,40},{56,48},{0,56},{9,1},... | collective-permute-start | bytes 6152 | tf_op jit(solution)/shard_map/ppermute | solution.py:30
  120.3 5.4 collective-permute-start.33
  146.1 6.9 %collective-permute-start.40 = (f32[2]{0:T(128)S(1)}, f32[2]{0:T(128)S(1)}, u32[]{:S(2)}, u32[]{:S(2)}) collective-permute-start(f32[2]{0:T(128)S(1)} %multiply_reduce_fusion.5), channel_id=1, source_target_pairs={{0,8},{8,0},{16,24},{24,16},{32,40},{40,32},{48,56},{56,48},{1,9},... | collective-permute-start | bytes 32 | tf_op jit(solution)/shard_map/ppermute | solution.py:41
  168.6 9.7 %collective-permute-start.47 = (f32[1,2,1,256]{3,2,1,0:T(1,128)S(1)}, f32[1,2,1,256]{3,2,1,0:T(1,128)S(1)}, u32[]{:S(2)}, u32[]{:S(2)}) collective-permute-start(f32[1,2,1,256]{3,2,1,0:T(1,128)S(1)} %get-tuple-element.405), channel_id=1, source_target_pairs={{8,0},{16,8},{24,16},{32,24},{40,32},{48,40},{56,48},{0,56},{9,1},... | collective-permute-start | bytes 6152 | tf_op jit(solution)/shard_map/ppermute | solution.py:30
  179.1 8.4 %collective-permute-start.49 = (f32[1,2,66,1]{3,2,1,0:T(8,128)}, f32[1,2,66,1]{3,2,1,0:T(8,128)}, u32[]{:S(2)}, u32[]{:S(2)}) collective-permute-start(f32[1,2,66,1]{3,2,1,0:T(8,128)} %get-tuple-element.376), channel_id=1, source_target_pairs={{0,1},{1,2},{2,3},{3,4},{4,5},{5,6},{6,7},{7,0},{8,9},{9,10},{10,1... | collective-permute-start | bytes 1592 | tf_op jit(solution)/shard_map/ppermute | solution.py:27
  180.0 7.6 %collective-permute-start.48 = (f32[1,2,66,1]{3,2,1,0:T(8,128)}, f32[1,2,66,1]{3,2,1,0:T(8,128)}, u32[]{:S(2)}, u32[]{:S(2)}) collective-permute-start(f32[1,2,66,1]{3,2,1,0:T(8,128)} %get-tuple-element.375), channel_id=1, source_target_pairs={{1,0},{2,1},{3,2},{4,3},{5,4},{6,5},{7,6},{0,7},{9,8},{10,9},{11,1... | collective-permute-start | bytes 1592 | tf_op jit(solution)/shard_map/ppermute | solution.py:30
  207.4 9.6 %collective-permute-start.56 = (f32[1,2,1,256]{3,2,1,0:T(1,128)S(1)}, f32[1,2,1,256]{3,2,1,0:T(1,128)S(1)}, u32[]{:S(2)}, u32[]{:S(2)}) collective-permute-start(f32[1,2,1,256]{3,2,1,0:T(1,128)S(1)} %get-tuple-element.401), channel_id=1, source_target_pairs={{0,8},{8,16},{16,24},{24,32},{32,40},{40,48},{48,56},{56,0},{1,9},... | collective-permute-start | bytes 6152 | tf_op jit(solution)/shard_map/ppermute | solution.py:27
  238.4 15.0 %collective-permute-start.63 = (f32[5,2,4,66,1]{3,2,4,1,0:T(4,128)}, f32[5,2,4,66,1]{3,2,4,1,0:T(4,128)}, u32[]{:S(2)}, u32[]{:S(2)}) collective-permute-start(f32[5,2,4,66,1]{3,2,4,1,0:T(4,128)} %copy.20), channel_id=1, source_target_pairs={{0,1},{1,2},{2,3},{3,4},{4,5},{5,6},{6,7},{7,0},{8,9},{9,10},{10,1... | collective-permute-start | bytes 31688 | tf_op jit(solution)/shard_map/ppermute | solution.py:27
  240.9 15.0 %collective-permute-start.62 = (f32[5,2,4,66,1]{3,2,4,1,0:T(4,128)}, f32[5,2,4,66,1]{3,2,4,1,0:T(4,128)}, u32[]{:S(2)}, u32[]{:S(2)}) collective-permute-start(f32[5,2,4,66,1]{3,2,4,1,0:T(4,128)} %copy.18), channel_id=1, source_target_pairs={{1,0},{2,1},{3,2},{4,3},{5,4},{6,5},{7,6},{0,7},{9,8},{10,9},{11,1... | collective-permute-start | bytes 31688 | tf_op jit(solution)/shard_map/ppermute | solution.py:30
  270.6 7.3 %collective-permute-start.67 = (f32[2,2,66,1]{3,2,1,0:T(8,128)}, f32[2,2,66,1]{3,2,1,0:T(8,128)}, u32[]{:S(2)}, u32[]{:S(2)}) collective-permute-start(f32[2,2,66,1]{3,2,1,0:T(8,128)} %get-tuple-element.354), channel_id=1, source_target_pairs={{0,1},{1,2},{2,3},{3,4},{4,5},{5,6},{6,7},{7,0},{8,9},{9,10},{10,1... | collective-permute-start | bytes 3176 | tf_op jit(solution)/shard_map/ppermute | solution.py:27
  270.6 7.3 %collective-permute-start.66 = (f32[2,2,66,1]{3,2,1,0:T(8,128)}, f32[2,2,66,1]{3,2,1,0:T(8,128)}, u32[]{:S(2)}, u32[]{:S(2)}) collective-permute-start(f32[2,2,66,1]{3,2,1,0:T(8,128)} %get-tuple-element.353), channel_id=1, source_target_pairs={{1,0},{2,1},{3,2},{4,3},{5,4},{6,5},{7,6},{0,7},{9,8},{10,9},{11,1... | collective-permute-start | bytes 3176 | tf_op jit(solution)/shard_map/ppermute | solution.py:30
  284.8 7.5 %collective-permute-start.77 = (f32[1,2,66,1]{3,2,1,0:T(8,128)}, f32[1,2,66,1]{3,2,1,0:T(8,128)}, u32[]{:S(2)}, u32[]{:S(2)}) collective-permute-start(f32[1,2,66,1]{3,2,1,0:T(8,128)} %get-tuple-element.372), channel_id=1, source_target_pairs={{0,1},{1,2},{2,3},{3,4},{4,5},{5,6},{6,7},{7,0},{8,9},{9,10},{10,1... | collective-permute-start | bytes 1592 | tf_op jit(solution)/shard_map/ppermute | solution.py:27
  284.8 8.1 %collective-permute-start.76 = (f32[1,2,66,1]{3,2,1,0:T(8,128)}, f32[1,2,66,1]{3,2,1,0:T(8,128)}, u32[]{:S(2)}, u32[]{:S(2)}) collective-permute-start(f32[1,2,66,1]{3,2,1,0:T(8,128)} %get-tuple-element.371), channel_id=1, source_target_pairs={{1,0},{2,1},{3,2},{4,3},{5,4},{6,5},{7,6},{0,7},{9,8},{10,9},{11,1... | collective-permute-start | bytes 1592 | tf_op jit(solution)/shard_map/ppermute | solution.py:30
  316.1 7.3 %collective-permute-start.84 = (f32[2]{0:T(128)S(1)}, f32[2]{0:T(128)S(1)}, u32[]{:S(2)}, u32[]{:S(2)}) collective-permute-start(f32[2]{0:T(128)S(1)} %get-tuple-element.307), channel_id=1, source_target_pairs={{0,8},{8,0},{16,24},{24,16},{32,40},{40,32},{48,56},{56,48},{1,9},... | collective-permute-start | bytes 32 | tf_op jit(solution)/shard_map/ppermute | solution.py:41
  339.0 7.5 %collective-permute-start.91 = (f32[1,2,1,256]{3,2,1,0:T(1,128)S(1)}, f32[1,2,1,256]{3,2,1,0:T(1,128)S(1)}, u32[]{:S(2)}, u32[]{:S(2)}) collective-permute-start(f32[1,2,1,256]{3,2,1,0:T(1,128)S(1)} %get-tuple-element.395), channel_id=1, source_target_pairs={{8,0},{16,8},{24,16},{32,24},{40,32},{48,40},{56,48},{0,56},{9,1},... | collective-permute-start | bytes 6152 | tf_op jit(solution)/shard_map/ppermute | solution.py:30
  347.2 8.1 %collective-permute-start.93 = (f32[1,2,66,1]{3,2,1,0:T(8,128)}, f32[1,2,66,1]{3,2,1,0:T(8,128)}, u32[]{:S(2)}, u32[]{:S(2)}) collective-permute-start(f32[1,2,66,1]{3,2,1,0:T(8,128)} %get-tuple-element.370), channel_id=1, source_target_pairs={{0,1},{1,2},{2,3},{3,4},{4,5},{5,6},{6,7},{7,0},{8,9},{9,10},{10,1... | collective-permute-start | bytes 1592 | tf_op jit(solution)/shard_map/ppermute | solution.py:27
  348.2 7.1 %collective-permute-start.92 = (f32[1,2,66,1]{3,2,1,0:T(8,128)}, f32[1,2,66,1]{3,2,1,0:T(8,128)}, u32[]{:S(2)}, u32[]{:S(2)}) collective-permute-start(f32[1,2,66,1]{3,2,1,0:T(8,128)} %get-tuple-element.369), channel_id=1, source_target_pairs={{1,0},{2,1},{3,2},{4,3},{5,4},{6,5},{7,6},{0,7},{9,8},{10,9},{11,1... | collective-permute-start | bytes 1592 | tf_op jit(solution)/shard_map/ppermute | solution.py:30
  377.6 6.9 %collective-permute-start.100 = (f32[2]{0:T(128)S(1)}, f32[2]{0:T(128)S(1)}, u32[]{:S(2)}, u32[]{:S(2)}) collective-permute-start(f32[2]{0:T(128)S(1)} %multiply_reduce_fusion), channel_id=1, source_target_pairs={{0,8},{8,0},{16,24},{24,16},{32,40},{40,32},{48,56},{56,48},{1,9},... | collective-permute-start | bytes 32 | tf_op jit(solution)/shard_map/ppermute | solution.py:41
  401.6 6.9 %collective-permute-start.107 = (f32[1,2,1,256]{3,2,1,0:T(1,128)S(1)}, f32[1,2,1,256]{3,2,1,0:T(1,128)S(1)}, u32[]{:S(2)}, u32[]{:S(2)}) collective-permute-start(f32[1,2,1,256]{3,2,1,0:T(1,128)S(1)} %get-tuple-element.391), channel_id=1, source_target_pairs={{8,0},{16,8},{24,16},{32,24},{40,32},{48,40},{56,48},{0,56},{9,1},... | collective-permute-start | bytes 6152 | tf_op jit(solution)/shard_map/ppermute | solution.py:30
  409.6 8.1 %collective-permute-start.109 = (f32[1,2,66,1]{3,2,1,0:T(8,128)}, f32[1,2,66,1]{3,2,1,0:T(8,128)}, u32[]{:S(2)}, u32[]{:S(2)}) collective-permute-start(f32[1,2,66,1]{3,2,1,0:T(8,128)} %get-tuple-element.368), channel_id=1, source_target_pairs={{0,1},{1,2},{2,3},{3,4},{4,5},{5,6},{6,7},{7,0},{8,9},{9,10},{10,1... | collective-permute-start | bytes 1592 | tf_op jit(solution)/shard_map/ppermute | solution.py:27
  409.6 8.1 %collective-permute-start.108 = (f32[1,2,66,1]{3,2,1,0:T(8,128)}, f32[1,2,66,1]{3,2,1,0:T(8,128)}, u32[]{:S(2)}, u32[]{:S(2)}) collective-permute-start(f32[1,2,66,1]{3,2,1,0:T(8,128)} %get-tuple-element.367), channel_id=1, source_target_pairs={{1,0},{2,1},{3,2},{4,3},{5,4},{6,5},{7,6},{0,7},{9,8},{10,9},{11,1... | collective-permute-start | bytes 1592 | tf_op jit(solution)/shard_map/ppermute | solution.py:30
  440.4 6.9 %collective-permute-start.117 = (f32[1,2,1,256]{3,2,1,0:T(1,128)S(1)}, f32[1,2,1,256]{3,2,1,0:T(1,128)S(1)}, u32[]{:S(2)}, u32[]{:S(2)}) collective-permute-start(f32[1,2,1,256]{3,2,1,0:T(1,128)S(1)} %get-tuple-element.388), channel_id=1, source_target_pairs={{8,0},{16,8},{24,16},{32,24},{40,32},{48,40},{56,48},{0,56},{9,1},... | collective-permute-start | bytes 6152 | tf_op jit(solution)/shard_map/ppermute | solution.py:30
  469.1 8.9 %collective-permute-start.122 = (f32[2,4,64]{2,1,0:T(4,128)S(1)}, f32[2,4,64]{2,1,0:T(4,128)S(1)}, u32[]{:S(2)}, u32[]{:S(2)}) collective-permute-start(f32[2,4,64]{2,1,0:T(4,128)S(1)} %add.751), channel_id=1, source_target_pairs={{0,4},{1,5},{2,6},{3,7},{4,0},{5,1},{6,2},{7,3},{8,12},{9,13},{10,... | collective-permute-start | bytes 6152 | tf_op jit(solution)/shard_map/ppermute | solution.py:41
  478.6 10.1 %collective-permute-start.123 = (f32[2]{0:T(128)S(1)}, f32[2]{0:T(128)S(1)}, u32[]{:S(2)}, u32[]{:S(2)}) collective-permute-start(f32[2]{0:T(128)S(1)} %broadcast_multiply_fusion.9), channel_id=1, source_target_pairs={{0,8},{8,0},{16,24},{24,16},{32,40},{40,32},{48,56},{56,48},{1,9},... | collective-permute-start | bytes 32 | tf_op jit(solution)/shard_map/ppermute | solution.py:41
  (149 other events, 803.5 us)
Sparse Core Ops, SparseCore 0:
  464.0 64.6 all-gather.1
where the time goes:
time: 553 us; the launch traced here: 543 us
  starting transfers between devices  207 us (37%)
  waiting for transfers between devices  172 us (31%)
  other arithmetic  72 us (13%)
  local copies, waits for them, and re-layouts  63.5 us (11%)
  between operations  16.6 us (3%)
  blocking collectives  11.7 us (2%)
    ppermute x78, waiting for transfers between devices, tree_sum(): values = values + lax.ppermute(values, axis, pairs)  128 us
    ppermute x78, starting transfers between devices, tree_sum(): values = values + lax.ppermute(values, axis, pairs)  104 us
    ppermute x24, starting transfers between devices, padded_2(): lax.ppermute(lax.slice_in_dim(block, 0, width, axis=dim), axis, backward)  91.6 us
    all_gather x1, waiting for transfers between devices, shards(): lax.all_gather(state_stack, 'member', axis=1, tiled=True)  23.3 us
    another operation x12, local copies, waits for them, and re-layouts, split_rims(): south_side = south_side.at[..., 0, :].multiply(south_keep)  13.3 us
    slice x22, local copies, waits for them, and re-layouts, padded_2(): lax.slice_in_dim(block, 0, width, axis=dim)  12.8 us
    ppermute x24, starting transfers between devices, padded_2(): lax.ppermute(lax.slice_in_dim(block, block.shape[dim] - width, None, axis...  12.2 us
    another operation x12, local copies, waits for them, and re-layouts, split_rims(): north_side = north_side.at[..., -1, :].multiply(north_keep)  11.5 us
  transfers between devices with their start and end apart: 127, of which 99 were waited for; matrix products, arithmetic and copies ran while one was open for 11% of the time, Pallas kernels for 0%

commit v1 on v0

--- a/solution.py
+++ b/solution.py
@@ -16,6 +16,11 @@
 SURF_C = 4.0
 DIV_K = 0.5
 GRAV_K = 0.5
+
+
+def exchange_gather(x, mesh_axis, dim):
+    sent = jnp.stack([x] * lax.axis_size(mesh_axis))
+    return jnp.concatenate(lax.all_to_all(sent, mesh_axis, 0, 0), axis=dim)
 
 
 def padded_2(block, sides, width):
@@ -167,7 +172,7 @@
     score = tree_sum(jnp.sum(overturn * lat_weight, axis=(1, 2)) * score_scale, ("gridy",))
     state_stack = jnp.stack((temp, salt, uvel, vvel))
     every_state, every_eta, every_score = (
-        lax.all_gather(state_stack, "member", axis=1, tiled=True),
+        exchange_gather(state_stack, "member", 1),
         lax.all_gather(eta, "member", axis=0, tiled=True),
         lax.all_gather(score, "member", axis=0, tiled=True),
     )

time: 553 us -> 722 us (1.31)
  other arithmetic: 72 us -> 190 us
  local copies, waits for them, and re-layouts: 63.5 us -> 92.9 us
  starting transfers between devices: 207 us -> 233 us
  between operations: 16.6 us -> 3.15 us
    another operation x2 -> x4, other arithmetic: 0.39 us -> 79.9 us  [pressure(): return PRESS_K * jnp.cumsum(BETA_S * salt - ALPHA_T * temp, axis=-3)]
    all_gather x1 -> x0, waiting for transfers between devices: 23.3 us -> none  [shards(): lax.all_gather(state_stack, 'member', axis=1, tiled=True)]
    ppermute x24, waiting for transfers between devices: 10.5 us -> 32.9 us  [padded_2(): lax.ppermute(lax.slice_in_dim(block, 0, width, axis=dim), axis, backward)]
    ppermute x78, starting transfers between devices: 104 us -> 119 us  [tree_sum(): values = values + lax.ppermute(values, axis, pairs)]
    ppermute x78, waiting for transfers between devices: 128 us -> 142 us  [tree_sum(): values = values + lax.ppermute(values, axis, pairs)]
    another operation x12 -> x10, local copies, waits for them, and re-layouts: 11.5 us -> 19.7 us  [split_rims(): north_side = north_side.at[..., -1, :].multiply(north_keep)]
    ppermute x24, waiting for transfers between devices: 10.2 us -> 2.95 us  [padded_2(): lax.ppermute(lax.slice_in_dim(block, block.shape[dim] - width, None, axis...]
    another operation x12 -> x10, local copies, waits for them, and re-layouts: 13.3 us -> 17.3 us  [split_rims(): south_side = south_side.at[..., 0, :].multiply(south_keep)]
  transfers between devices with their start and end apart: 127 -> 127, of which waited for: 99 -> 93; matrix products, arithmetic and copies ran while one was open for 11% -> 17% of each run, Pallas kernels for 0% -> 0%
where the time goes in v1:
time: 722 us; the launch traced here: 709 us
  starting transfers between devices  233 us (32%)
  other arithmetic  190 us (26%)
  waiting for transfers between devices  178 us (25%)
  local copies, waits for them, and re-layouts  92.9 us (13%)
  blocking collectives  11.7 us (2%)
    ppermute x78, waiting for transfers between devices, tree_sum(): values = values + lax.ppermute(values, axis, pairs)  142 us
    ppermute x78, starting transfers between devices, tree_sum(): values = values + lax.ppermute(values, axis, pairs)  119 us
    ppermute x24, starting transfers between devices, padded_2(): lax.ppermute(lax.slice_in_dim(block, 0, width, axis=dim), axis, backward)  95.2 us
    another operation x4, other arithmetic, pressure(): return PRESS_K * jnp.cumsum(BETA_S * salt - ALPHA_T * temp, axis=-3)  79.9 us
    ppermute x24, waiting for transfers between devices, padded_2(): lax.ppermute(lax.slice_in_dim(block, 0, width, axis=dim), axis, backward)  32.9 us
    another operation x10, local copies, waits for them, and re-layouts, split_rims(): north_side = north_side.at[..., -1, :].multiply(north_keep)  19.7 us
    another operation x10, local copies, waits for them, and re-layouts, split_rims(): south_side = south_side.at[..., 0, :].multiply(south_keep)  17.3 us
  transfers between devices with their start and end apart: 127, of which 93 were waited for; matrix products, arithmetic and copies ran while one was open for 17% of the time, Pallas kernels for 0%

profile of v1, /device:TPU:1, one launch (start us, length us, event | category | flops | bytes accessed | tf_op | source)
XLA Modules:
  0.0 709.2 jit_solution(9211693679718649728)
XLA Ops:
  6.1 35.3 %reduce_window_sum.33 = f32[1,2,4,64,256]{4,2,3,1,0:T(4,128)} reduce-window(f32[1,2,4,64,256]{4,2,3,1,0:T(4,128)} %subtract_bitcast_fusion.1, f32[]{:T(128)} %constant.599.clone.1), window={size=1x1x4x1x1 pad=0_0x0_0x3_0x0_0x0_0}, to_apply=%region_0.0 | reduce-window | flops 393216 | bytes 1048580 | tf_op jit(solution)/shard_map/jit(cumsum)/reduce_window_sum | solution.py:52
  66.1 5.4 fusion.172
  72.5 6.3 fusion.170
  81.8 4.2 collective-permute-start.5
  108.9 4.3 collective-permute-start.15
  128.6 4.3 collective-permute-start.18
  149.3 6.1 collective-permute-start.24
  172.1 5.9 collective-permute-start.31
  179.3 6.5 subtract_bitcast_fusion
  209.0 6.0 collective-permute-start.40
  231.0 6.1 collective-permute-start.47
  273.7 5.9 collective-permute-start.56
  279.9 35.4 %reduce_window_sum.35 = f32[1,2,4,64,256]{4,2,3,1,0:T(4,128)} reduce-window(f32[1,2,4,64,256]{4,2,3,1,0:T(4,128)} %get-tuple-element.323, f32[]{:T(128)} %constant.599.clone.1), window={size=1x1x4x1x1 pad=0_0x0_0x3_0x0_0x0_0}, to_apply=%region_9.10 | reduce-window | flops 393216 | bytes 1048580 | tf_op jit(solution)/shard_map/jit(cumsum)/reduce_window_sum | solution.py:52
  361.8 4.8 fusion.162
  368.3 5.8 fusion.160
  380.3 5.9 collective-permute-done.65
  401.2 4.3 collective-permute-start.75
  421.2 4.3 collective-permute-start.78
  441.9 6.0 collective-permute-start.84
  464.5 6.0 collective-permute-start.91
  471.9 4.3 collective-permute-done.91
  508.0 6.1 collective-permute-start.100
  532.2 6.1 collective-permute-start.107
  538.5 4.3 collective-permute-done.107
  575.9 6.1 collective-permute-start.117
  601.6 4.2 fusion.79
  613.2 5.7 all-to-all-start
  619.1 43.0 %collective-permute-done.120 = f32[2,4,64]{1,2,0:T(8,128)S(1)} collective-permute-done((f32[2,4,64]{1,2,0:T(8,128)S(1)}, f32[2,4,64]{1,2,0:T(8,128)S(1)}, u32[]{:S(2)}, u32[]{:S(2)}) %collective-permute-start.120) | collective-permute-done | bytes 2080 | tf_op jit(solution)/shard_map/ppermute | solution.py:46
  668.6 6.1 all_gather.6
  675.8 7.4 %collective-permute-start.123 = (f32[2]{0:T(128)S(1)}, f32[2]{0:T(128)S(1)}, u32[]{:S(2)}, u32[]{:S(2)}) collective-permute-start(f32[2]{0:T(128)S(1)} %broadcast_multiply_fusion.5), channel_id=1, source_target_pairs={{0,8},{8,0},{16,24},{24,16},{32,40},{40,32},{48,56},{56,48},{1,9},... | collective-permute-start | bytes 32 | tf_op jit(solution)/shard_map/ppermute | solution.py:46
  691.1 5.6 all-reduce
  699.8 4.8 copy.544
  (564 shorter events, 433.8 us)
Async XLA Ops:
  52.0 10.7 %collective-permute-start.3 = (f32[5,2,4,66,1]{3,2,4,1,0:T(4,128)S(1)}, f32[5,2,4,66,1]{3,2,4,1,0:T(4,128)S(1)}, u32[]{:S(2)}, u32[]{:S(2)}) collective-permute-start(f32[5,2,4,66,1]{3,2,4,1,0:T(4,128)S(1)} %copy.454), channel_id=1, source_target_pairs={{0,1},{1,2},{2,3},{3,4},{4,5},{5,6},{6,7},{7,0},{8,9},{9,10},{10,1... | collective-permute-start | bytes 31688 | tf_op jit(solution)/shard_map/ppermute | solution.py:32
  55.2 9.2 %collective-permute-start.2 = (f32[5,2,4,66,1]{3,2,4,1,0:T(4,128)S(1)}, f32[5,2,4,66,1]{3,2,4,1,0:T(4,128)S(1)}, u32[]{:S(2)}, u32[]{:S(2)}) collective-permute-start(f32[5,2,4,66,1]{3,2,4,1,0:T(4,128)S(1)} %copy.452), channel_id=1, source_target_pairs={{1,0},{2,1},{3,2},{4,3},{5,4},{6,5},{7,6},{0,7},{9,8},{10,9},{11,1... | collective-permute-start | bytes 31688 | tf_op jit(solution)/shard_map/ppermute | solution.py:35
  81.8 9.4 %collective-permute-start.5 = (f32[2,2,1,256]{2,3,1,0:T(8,128)}, f32[2,2,1,256]{2,3,1,0:T(8,128)S(1)}, u32[]{:S(2)}, u32[]{:S(2)}) collective-permute-start(f32[2,2,1,256]{2,3,1,0:T(8,128)} %get-tuple-element.391), channel_id=1, source_target_pairs={{8,0},{16,8},{24,16},{32,24},{40,32},{48,40},{56,48},{0,56},{9,1},... | collective-permute-start | bytes 12296 | tf_op jit(solution)/shard_map/ppermute | solution.py:35
  93.9 13.1 %collective-permute-start.7 = (f32[2,2,66,1]{2,3,1,0:T(1,128)}, f32[2,2,66,1]{2,3,1,0:T(1,128)}, u32[]{:S(2)}, u32[]{:S(2)}) collective-permute-start(f32[2,2,66,1]{2,3,1,0:T(1,128)} %get-tuple-element.360), channel_id=1, source_target_pairs={{0,1},{1,2},{2,3},{3,4},{4,5},{5,6},{6,7},{7,0},{8,9},{9,10},{10,1... | collective-permute-start | bytes 3176 | tf_op jit(solution)/shard_map/ppermute | solution.py:32
  93.9 13.1 %collective-permute-start.6 = (f32[2,2,66,1]{2,3,1,0:T(1,128)}, f32[2,2,66,1]{2,3,1,0:T(1,128)}, u32[]{:S(2)}, u32[]{:S(2)}) collective-permute-start(f32[2,2,66,1]{2,3,1,0:T(1,128)} %get-tuple-element.359), channel_id=1, source_target_pairs={{1,0},{2,1},{3,2},{4,3},{5,4},{6,5},{7,6},{0,7},{9,8},{10,9},{11,1... | collective-permute-start | bytes 3176 | tf_op jit(solution)/shard_map/ppermute | solution.py:35
  117.1 9.9 %collective-permute-start.17 = (f32[1,2,66,1]{2,3,1,0:T(1,128)}, f32[1,2,66,1]{2,3,1,0:T(1,128)}, u32[]{:S(2)}, u32[]{:S(2)}) collective-permute-start(f32[1,2,66,1]{2,3,1,0:T(1,128)} %get-tuple-element.376), channel_id=1, source_target_pairs={{0,1},{1,2},{2,3},{3,4},{4,5},{5,6},{6,7},{7,0},{8,9},{9,10},{10,1... | collective-permute-start | bytes 1592 | tf_op jit(solution)/shard_map/ppermute | solution.py:32
  117.1 9.9 %collective-permute-start.16 = (f32[1,2,66,1]{2,3,1,0:T(1,128)}, f32[1,2,66,1]{2,3,1,0:T(1,128)}, u32[]{:S(2)}, u32[]{:S(2)}) collective-permute-start(f32[1,2,66,1]{2,3,1,0:T(1,128)} %get-tuple-element.375), channel_id=1, source_target_pairs={{1,0},{2,1},{3,2},{4,3},{5,4},{6,5},{7,6},{0,7},{9,8},{10,9},{11,1... | collective-permute-start | bytes 1592 | tf_op jit(solution)/shard_map/ppermute | solution.py:35
  172.1 13.7 %collective-permute-start.31 = (f32[1,2,1,256]{2,3,1,0:T(8,128)S(1)}, f32[1,2,1,256]{2,3,1,0:T(8,128)S(1)}, u32[]{:S(2)}, u32[]{:S(2)}) collective-permute-start(f32[1,2,1,256]{2,3,1,0:T(8,128)S(1)} %get-tuple-element.415), channel_id=1, source_target_pairs={{8,0},{16,8},{24,16},{32,24},{40,32},{48,40},{56,48},{0,56},{9,1},... | collective-permute-start | bytes 6152 | tf_op jit(solution)/shard_map/ppermute | solution.py:35
  178.0 7.8 %collective-permute-start.30 = (f32[1,2,1,256]{2,3,1,0:T(8,128)S(1)}, f32[1,2,1,256]{2,3,1,0:T(8,128)S(1)}, u32[]{:S(2)}, u32[]{:S(2)}) collective-permute-start(f32[1,2,1,256]{2,3,1,0:T(8,128)S(1)} %get-tuple-element.416), channel_id=1, source_target_pairs={{0,8},{8,16},{16,24},{24,32},{32,40},{40,48},{48,56},{56,0},{1,9},... | collective-permute-start | bytes 6152 | tf_op jit(solution)/shard_map/ppermute | solution.py:32
  231.0 11.5 %collective-permute-start.47 = (f32[1,2,1,256]{2,3,1,0:T(8,128)S(1)}, f32[1,2,1,256]{2,3,1,0:T(8,128)S(1)}, u32[]{:S(2)}, u32[]{:S(2)}) collective-permute-start(f32[1,2,1,256]{2,3,1,0:T(8,128)S(1)} %get-tuple-element.411), channel_id=1, source_target_pairs={{8,0},{16,8},{24,16},{32,24},{40,32},{48,40},{56,48},{0,56},{9,1},... | collective-permute-start | bytes 6152 | tf_op jit(solution)/shard_map/ppermute | solution.py:35
  242.6 10.4 %collective-permute-start.49 = (f32[1,2,66,1]{2,3,1,0:T(1,128)S(1)}, f32[1,2,66,1]{2,3,1,0:T(1,128)S(1)}, u32[]{:S(2)}, u32[]{:S(2)}) collective-permute-start(f32[1,2,66,1]{2,3,1,0:T(1,128)S(1)} %get-tuple-element.372), channel_id=1, source_target_pairs={{0,1},{1,2},{2,3},{3,4},{4,5},{5,6},{6,7},{7,0},{8,9},{9,10},{10,1... | collective-permute-start | bytes 1592 | tf_op jit(solution)/shard_map/ppermute | solution.py:32
  242.6 10.3 %collective-permute-start.48 = (f32[1,2,66,1]{2,3,1,0:T(1,128)S(1)}, f32[1,2,66,1]{2,3,1,0:T(1,128)S(1)}, u32[]{:S(2)}, u32[]{:S(2)}) collective-permute-start(f32[1,2,66,1]{2,3,1,0:T(1,128)S(1)} %get-tuple-element.371), channel_id=1, source_target_pairs={{1,0},{2,1},{3,2},{4,3},{5,4},{6,5},{7,6},{0,7},{9,8},{10,9},{11,1... | collective-permute-start | bytes 1592 | tf_op jit(solution)/shard_map/ppermute | solution.py:35
  273.7 41.5 %collective-permute-start.56 = (f32[1,2,1,256]{2,3,1,0:T(8,128)}, f32[1,2,1,256]{2,3,1,0:T(8,128)S(1)}, u32[]{:S(2)}, u32[]{:S(2)}) collective-permute-start(f32[1,2,1,256]{2,3,1,0:T(8,128)} %get-tuple-element.407), channel_id=1, source_target_pairs={{0,8},{8,16},{16,24},{24,32},{32,40},{40,48},{48,56},{56,0},{1,9},... | collective-permute-start | bytes 6152 | tf_op jit(solution)/shard_map/ppermute | solution.py:32
  279.6 35.6 %collective-permute-start.57 = (f32[1,2,1,256]{2,3,1,0:T(8,128)}, f32[1,2,1,256]{2,3,1,0:T(8,128)S(1)}, u32[]{:S(2)}, u32[]{:S(2)}) collective-permute-start(f32[1,2,1,256]{2,3,1,0:T(8,128)} %get-tuple-element.408), channel_id=1, source_target_pairs={{8,0},{16,8},{24,16},{32,24},{40,32},{48,40},{56,48},{0,56},{9,1},... | collective-permute-start | bytes 6152 | tf_op jit(solution)/shard_map/ppermute | solution.py:35
  346.3 10.7 %collective-permute-start.63 = (f32[5,2,4,66,1]{3,2,4,1,0:T(4,128)}, f32[5,2,4,66,1]{3,2,4,1,0:T(4,128)}, u32[]{:S(2)}, u32[]{:S(2)}) collective-permute-start(f32[5,2,4,66,1]{3,2,4,1,0:T(4,128)} %copy.511), channel_id=1, source_target_pairs={{0,1},{1,2},{2,3},{3,4},{4,5},{5,6},{6,7},{7,0},{8,9},{9,10},{10,1... | collective-permute-start | bytes 31688 | tf_op jit(solution)/shard_map/ppermute | solution.py:32
  348.7 10.7 %collective-permute-start.62 = (f32[5,2,4,66,1]{3,2,4,1,0:T(4,128)}, f32[5,2,4,66,1]{3,2,4,1,0:T(4,128)}, u32[]{:S(2)}, u32[]{:S(2)}) collective-permute-start(f32[5,2,4,66,1]{3,2,4,1,0:T(4,128)} %copy.509), channel_id=1, source_target_pairs={{1,0},{2,1},{3,2},{4,3},{5,4},{6,5},{7,6},{0,7},{9,8},{10,9},{11,1... | collective-permute-start | bytes 31688 | tf_op jit(solution)/shard_map/ppermute | solution.py:35
  376.6 9.7 %collective-permute-start.65 = (f32[2,2,1,256]{2,3,1,0:T(8,128)S(1)}, f32[2,2,1,256]{2,3,1,0:T(8,128)S(1)}, u32[]{:S(2)}, u32[]{:S(2)}) collective-permute-start(f32[2,2,1,256]{2,3,1,0:T(8,128)S(1)} %get-tuple-element.384), channel_id=1, source_target_pairs={{8,0},{16,8},{24,16},{32,24},{40,32},{48,40},{56,48},{0,56},{9,1},... | collective-permute-start | bytes 12296 | tf_op jit(solution)/shard_map/ppermute | solution.py:35
  388.0 11.1 %collective-permute-start.67 = (f32[2,2,66,1]{2,3,1,0:T(1,128)}, f32[2,2,66,1]{2,3,1,0:T(1,128)}, u32[]{:S(2)}, u32[]{:S(2)}) collective-permute-start(f32[2,2,66,1]{2,3,1,0:T(1,128)} %get-tuple-element.358), channel_id=1, source_target_pairs={{0,1},{1,2},{2,3},{3,4},{4,5},{5,6},{6,7},{7,0},{8,9},{9,10},{10,1... | collective-permute-start | bytes 3176 | tf_op jit(solution)/shard_map/ppermute | solution.py:32
  388.0 11.1 %collective-permute-start.66 = (f32[2,2,66,1]{2,3,1,0:T(1,128)}, f32[2,2,66,1]{2,3,1,0:T(1,128)}, u32[]{:S(2)}, u32[]{:S(2)}) collective-permute-start(f32[2,2,66,1]{2,3,1,0:T(1,128)} %get-tuple-element.357), channel_id=1, source_target_pairs={{1,0},{2,1},{3,2},{4,3},{5,4},{6,5},{7,6},{0,7},{9,8},{10,9},{11,1... | collective-permute-start | bytes 3176 | tf_op jit(solution)/shard_map/ppermute | solution.py:35
  409.5 10.3 %collective-permute-start.77 = (f32[1,2,66,1]{2,3,1,0:T(1,128)}, f32[1,2,66,1]{2,3,1,0:T(1,128)}, u32[]{:S(2)}, u32[]{:S(2)}) collective-permute-start(f32[1,2,66,1]{2,3,1,0:T(1,128)} %get-tuple-element.368), channel_id=1, source_target_pairs={{0,1},{1,2},{2,3},{3,4},{4,5},{5,6},{6,7},{7,0},{8,9},{9,10},{10,1... | collective-permute-start | bytes 1592 | tf_op jit(solution)/shard_map/ppermute | solution.py:32
  409.5 10.3 %collective-permute-start.76 = (f32[1,2,66,1]{2,3,1,0:T(1,128)}, f32[1,2,66,1]{2,3,1,0:T(1,128)}, u32[]{:S(2)}, u32[]{:S(2)}) collective-permute-start(f32[1,2,66,1]{2,3,1,0:T(1,128)} %get-tuple-element.367), channel_id=1, source_target_pairs={{1,0},{2,1},{3,2},{4,3},{5,4},{6,5},{7,6},{0,7},{9,8},{10,9},{11,1... | collective-permute-start | bytes 1592 | tf_op jit(solution)/shard_map/ppermute | solution.py:35
  464.5 11.8 %collective-permute-start.91 = (f32[1,2,1,256]{2,3,1,0:T(8,128)S(1)}, f32[1,2,1,256]{2,3,1,0:T(8,128)S(1)}, u32[]{:S(2)}, u32[]{:S(2)}) collective-permute-start(f32[1,2,1,256]{2,3,1,0:T(8,128)S(1)} %get-tuple-element.401), channel_id=1, source_target_pairs={{8,0},{16,8},{24,16},{32,24},{40,32},{48,40},{56,48},{0,56},{9,1},... | collective-permute-start | bytes 6152 | tf_op jit(solution)/shard_map/ppermute | solution.py:35
  476.9 10.0 %collective-permute-start.93 = (f32[1,2,66,1]{2,3,1,0:T(1,128)}, f32[1,2,66,1]{2,3,1,0:T(1,128)}, u32[]{:S(2)}, u32[]{:S(2)}) collective-permute-start(f32[1,2,66,1]{2,3,1,0:T(1,128)} %get-tuple-element.366), channel_id=1, source_target_pairs={{0,1},{1,2},{2,3},{3,4},{4,5},{5,6},{6,7},{7,0},{8,9},{9,10},{10,1... | collective-permute-start | bytes 1592 | tf_op jit(solution)/shard_map/ppermute | solution.py:32
  476.9 10.0 %collective-permute-start.92 = (f32[1,2,66,1]{2,3,1,0:T(1,128)}, f32[1,2,66,1]{2,3,1,0:T(1,128)}, u32[]{:S(2)}, u32[]{:S(2)}) collective-permute-start(f32[1,2,66,1]{2,3,1,0:T(1,128)} %get-tuple-element.365), channel_id=1, source_target_pairs={{1,0},{2,1},{3,2},{4,3},{5,4},{6,5},{7,6},{0,7},{9,8},{10,9},{11,1... | collective-permute-start | bytes 1592 | tf_op jit(solution)/shard_map/ppermute | solution.py:35
  532.2 10.6 %collective-permute-start.107 = (f32[1,2,1,256]{2,3,1,0:T(8,128)S(1)}, f32[1,2,1,256]{2,3,1,0:T(8,128)S(1)}, u32[]{:S(2)}, u32[]{:S(2)}) collective-permute-start(f32[1,2,1,256]{2,3,1,0:T(8,128)S(1)} %get-tuple-element.397), channel_id=1, source_target_pairs={{8,0},{16,8},{24,16},{32,24},{40,32},{48,40},{56,48},{0,56},{9,1},... | collective-permute-start | bytes 6152 | tf_op jit(solution)/shard_map/ppermute | solution.py:35
  543.6 10.1 %collective-permute-start.109 = (f32[1,2,66,1]{2,3,1,0:T(1,128)}, f32[1,2,66,1]{2,3,1,0:T(1,128)}, u32[]{:S(2)}, u32[]{:S(2)}) collective-permute-start(f32[1,2,66,1]{2,3,1,0:T(1,128)} %get-tuple-element.364), channel_id=1, source_target_pairs={{0,1},{1,2},{2,3},{3,4},{4,5},{5,6},{6,7},{7,0},{8,9},{9,10},{10,1... | collective-permute-start | bytes 1592 | tf_op jit(solution)/shard_map/ppermute | solution.py:32
  543.7 10.0 %collective-permute-start.108 = (f32[1,2,66,1]{2,3,1,0:T(1,128)}, f32[1,2,66,1]{2,3,1,0:T(1,128)}, u32[]{:S(2)}, u32[]{:S(2)}) collective-permute-start(f32[1,2,66,1]{2,3,1,0:T(1,128)} %get-tuple-element.363), channel_id=1, source_target_pairs={{1,0},{2,1},{3,2},{4,3},{5,4},{6,5},{7,6},{0,7},{9,8},{10,9},{11,1... | collective-permute-start | bytes 1592 | tf_op jit(solution)/shard_map/ppermute | solution.py:35
  575.9 10.0 %collective-permute-start.117 = (f32[1,2,1,256]{2,3,1,0:T(8,128)S(1)}, f32[1,2,1,256]{2,3,1,0:T(8,128)S(1)}, u32[]{:S(2)}, u32[]{:S(2)}) collective-permute-start(f32[1,2,1,256]{2,3,1,0:T(8,128)S(1)} %get-tuple-element.394), channel_id=1, source_target_pairs={{8,0},{16,8},{24,16},{32,24},{40,32},{48,40},{56,48},{0,56},{9,1},... | collective-permute-start | bytes 6152 | tf_op jit(solution)/shard_map/ppermute | solution.py:35
  613.2 86.6 %all-to-all-start = ((f32[2,4,2,4,64,256]{5,4,3,2,1,0:T(8,128)}), f32[2,4,2,4,64,256]{5,4,3,2,1,0:T(8,128)}, u32[]{:S(2)}, u32[]{:S(2)}) async-start(f32[2,4,2,4,64,256]{5,4,3,2,1,0:T(8,128)} %copy.543), calls=%async_computation | async-start | bytes 8388608 | tf_op jit(solution)/shard_map/all_to_all | solution.py:23
  618.9 43.1 %collective-permute-start.120 = (f32[2,4,64]{1,2,0:T(8,128)S(1)}, f32[2,4,64]{1,2,0:T(8,128)S(1)}, u32[]{:S(2)}, u32[]{:S(2)}) collective-permute-start(f32[2,4,64]{1,2,0:T(8,128)S(1)} %copy-done.41), channel_id=1, source_target_pairs={{0,1},{1,0},{2,3},{3,2},{4,5},{5,4},{6,7},{7,6},{8,9},{9,8},{10,11... | collective-permute-start | bytes 6152 | tf_op jit(solution)/shard_map/ppermute | solution.py:46
  665.7 9.6 %collective-permute-start.122 = (f32[2,4,64]{1,2,0:T(8,128)S(1)}, f32[2,4,64]{1,2,0:T(8,128)S(1)}, u32[]{:S(2)}, u32[]{:S(2)}) collective-permute-start(f32[2,4,64]{1,2,0:T(8,128)S(1)} %add.751), channel_id=1, source_target_pairs={{0,4},{1,5},{2,6},{3,7},{4,0},{5,1},{6,2},{7,3},{8,12},{9,13},{10,... | collective-permute-start | bytes 6152 | tf_op jit(solution)/shard_map/ppermute | solution.py:46
  675.8 8.2 %collective-permute-start.123 = (f32[2]{0:T(128)S(1)}, f32[2]{0:T(128)S(1)}, u32[]{:S(2)}, u32[]{:S(2)}) collective-permute-start(f32[2]{0:T(128)S(1)} %broadcast_multiply_fusion.5), channel_id=1, source_target_pairs={{0,8},{8,0},{16,24},{24,16},{32,40},{40,32},{48,56},{56,48},{1,9},... | collective-permute-start | bytes 32 | tf_op jit(solution)/shard_map/ppermute | solution.py:46
  (146 other events, 1135.1 us)
